TPU v7x, 128 devices: a whole 4x4x4 slice. The times are simulated.
128 devices in a mesh: group: 8 (over y, core), local: 16 (over z, x).
Axes of the slice: x: 4, y: 4, z: 4, core: 2. Of those that a mesh axis runs over, the one named last changes fastest.
Arguments:
- lookup_grads: bfloat16 [1048576, 256], P(('group', 'local')), may hold values from -0.29882812 to 0.29882812
- slot_index: int32 [2, 1048576], P(None, ('group', 'local')), may hold values from 0 to 2047, as said below
- unique_rows: int32 [2, 16384], P(None, ('group', 'local')), may hold values from -1 to 131071, as said below
- tables: float32 [2, 131072, 256], P(None, ('group', 'local')), may hold values from -6 to 6
- accums: float32 [2, 131072], P(None, ('group', 'local')), may hold values from 0.01 to 1
Outputs:
- new_tables: float32 [2, 131072, 256], P(None, ('group', 'local'))
- new_accums: float32 [2, 131072], P(None, ('group', 'local'))
Inputs may be any that keep to these rules, and one draw needn't show every extreme that they name: slot_index[t, i] names a slot of lookup i's group list whose entry in unique_rows[t] is not -1. `unique_rows`: table row p is owned by device p // 1024, which is device (group p // 16384, local p // 1024 % 16). Group g's list is entries g * 2048 to (g + 1) * 2048 - 1; its block l of 128 entries consists of 8 buckets of 16 entries, bucket h holding only rows owned by device (group h, local l), the used entries first and -1 after them. Rows within a group's list are distinct. In every draw and table some device (group h, local l) gets a full bucket from every group.
All inputs are finite; a program needn't handle non-finite values.
Results may differ from a plain program's by a relative error of at most 0.0003.
Values sent between devices are 32-bit elements; how exact they have to be, the bound alone decides.
No kernel may reach another device: no remote copies, remote signals or barrier semaphores. Data moves between devices by JAX's collectives and lax.ppermute only.
A program may use at most 64 MiB of HBM per device.

v0:
```python
import jax
import jax.numpy as jnp
from jax import lax
from jax.sharding import PartitionSpec as P

learning_rate = 0.1
epsilon = 1e-08


def slot_sums(lookup_grads, slot_index, row_count):
    block_len = min(2048, lookup_grads.shape[0])
    block_count = lookup_grads.shape[0] // block_len
    width = lookup_grads.shape[1]
    grad_blocks = lookup_grads.reshape(block_count, block_len, width)
    index_blocks = jnp.transpose(slot_index.reshape(2, block_count, block_len), (1, 0, 2))
    targets = lax.iota(jnp.int32, row_count)

    def accumulate(running, inputs):
        gradients, indices = inputs
        pieces = []
        for table_index in range(2):
            onehot = (indices[table_index][:, None] == targets[None, :]).astype(jnp.bfloat16)
            pieces.append(
                lax.dot_general(
                    onehot, gradients, (((0,), (0,)), ((), ())), preferred_element_type=jnp.float32
                )
            )
        return (running + jnp.concatenate(pieces, axis=1), None)

    start_sums = jnp.zeros((row_count, 2 * width), jnp.float32)
    summed, _ = lax.scan(accumulate, start_sums, (grad_blocks, index_blocks))
    return summed


def apply_update(summed, row_pairs, tables, accums):
    rows_dev = tables.shape[1]
    width = tables.shape[2]
    new_tables = []
    new_accums = []
    for table_index in range(2):
        row_numbers = row_pairs[:, table_index]
        local_rows = jnp.where(row_numbers < 0, rows_dev, row_numbers % rows_dev)
        values = summed[:, table_index * width : (table_index + 1) * width]
        row_grads = (
            jnp.zeros((rows_dev, width), jnp.float32).at[local_rows].add(values, mode="drop")
        )
        accum_new = accums[table_index] + jnp.mean(row_grads * row_grads, axis=1)
        table_new = tables[table_index] - learning_rate * row_grads / (
            jnp.sqrt(accum_new)[:, None] + epsilon
        )
        new_tables.append(table_new)
        new_accums.append(accum_new)
    return (jnp.stack(new_tables), jnp.stack(new_accums))


def local(lookup_grads, slot_index, unique_rows, tables, accums):
    n_group = lax.axis_size("group")
    n_local = lax.axis_size("local")
    slots = unique_rows.shape[1]
    capacity = slots // n_group
    width = lookup_grads.shape[1]
    row_pairs = jnp.transpose(unique_rows)
    own_sums = slot_sums(lookup_grads, slot_index, slots * n_local)
    ordered = own_sums.reshape(n_local, n_group, capacity, 2 * width)
    ordered = jnp.transpose(ordered, (1, 0, 2, 3)).reshape(n_local * slots, 2 * width)
    received = lax.all_to_all(ordered, ("group", "local"), split_axis=0, concat_axis=0, tiled=True)
    arrived = jnp.sum(received.reshape(n_group, n_local, capacity, 2 * width), axis=1).reshape(
        slots, 2 * width
    )
    arrived_rows = lax.all_to_all(row_pairs, "group", split_axis=0, concat_axis=0, tiled=True)
    return apply_update(arrived, arrived_rows, tables, accums)


def solution(mesh):
    return jax.shard_map(
        local,
        mesh=mesh,
        in_specs=(
            P(("group", "local"), None),
            P(None, ("group", "local")),
            P(None, ("group", "local")),
            P(None, ("group", "local"), None),
            P(None, ("group", "local")),
        ),
        out_specs=(P(None, ("group", "local"), None), P(None, ("group", "local"))),
        check_vma=False,
    )
```

profile of v0, /device:TPU:1, one launch (start us, length us, event | category | flops | bytes accessed | tf_op | source)
XLA Modules:
  0.0 159.0 jit_solution(276250633649171804)
XLA Ops:
  0.6 0.8 all_to_all.14
  1.4 0.6 copy.11
  2.0 6.0 %all-to-all-start = ((s32[8,16,2]{1,2,0:T(2,128)}), s32[8,16,2]{1,2,0:T(2,128)S(1)}, u32[]{:S(2)}, u32[]{:S(2)}) async-start(s32[8,16,2]{1,2,0:T(2,128)} %copy.11), calls=%async_computation | async-start | bytes 16384 | tf_op jit(solution)/shard_map/all_to_all | solution.py:70
  8.0 68.6 %while.12 = (s32[]{:T(128)}, f32[2048,512]{0,1:T(8,128)}, s32[4,2,2048]{2,1,0:T(2,128)}, bf16[4,2048,256]{2,1,0:T(8,128)(2,1)}, s32[]{:T(128)}, /*index=5*/s32[]{:T(128)}, s32[]{}) while((s32[]{:T(128)}, f32[2048,512]{0,1:T(8,128)}, s32[4,2,2048]{2,1,0:T(2,128)}, bf16[4,2048,256]{2,1,0:T(8,128)(2,1)}, s32[]{:T(128)}, ...), condition=%wide.region_1.2_spmd.clone.clone, body=%wide.region_0.1_spmd.clone.clone.sunk | while | flops 4306501632 | bytes 18924652 | solution.py:31
  8.0 0.8 constant_dynamic-slice_fusion.3
  8.8 4.8 %fusion.30 = f32[2048,256]{0,1:T(8,128)S(1)} fusion(s32[2048]{0:T(1024)S(1)} %bitcast.56, bf16[4,2048,256]{2,1,0:T(8,128)(2,1)} %get-tuple-element.130, s32[]{:T(128)} %get-tuple-element.120), kind=kOutput, calls=%fused_computation.6.clone.1 | convolution fusion | flops 2151677952 | bytes 3154432 | tf_op jit(solution)/shard_map/while/body/eval_jaxpr/dot_general | solution.py:24
  13.6 6.1 %fusion.31 = f32[2048,256]{0,1:T(8,128)} fusion(s32[2048]{0:T(1024)S(1)} %bitcast.55, bf16[4,2048,256]{2,1,0:T(8,128)(2,1)} %get-tuple-element.130, s32[]{:T(128)} %get-tuple-element.120), kind=kOutput, calls=%fused_computation.5.clone.1 | convolution fusion | flops 2151677952 | bytes 3154432 | tf_op jit(solution)/shard_map/while/body/eval_jaxpr/dot_general | solution.py:24
  19.7 4.5 %maximum_add_fusion.2 = f32[2048,512]{0,1:T(8,128)} fusion(f32[2048,256]{0,1:T(8,128)S(1)} %fusion.30, f32[2048,256]{0,1:T(8,128)} %fusion.31, f32[2048,512]{0,1:T(8,128)} %get-tuple-element.121, pred[]{:T(512)S(6)} %compare.5), kind=kLoop, calls=%fused_computation.9.clone.1 | loop fusion | flops 3145728 | bytes 12582913 | tf_op jit(solution)/shard_map/while/body/eval_jaxpr/add | solution.py:28
  24.2 0.8 constant_dynamic-slice_fusion.3
  25.0 4.8 %fusion.30 = f32[2048,256]{0,1:T(8,128)S(1)} fusion(s32[2048]{0:T(1024)S(1)} %bitcast.56, bf16[4,2048,256]{2,1,0:T(8,128)(2,1)} %get-tuple-element.130, s32[]{:T(128)} %get-tuple-element.120), kind=kOutput, calls=%fused_computation.6.clone.1 | convolution fusion | flops 2151677952 | bytes 3154432 | tf_op jit(solution)/shard_map/while/body/eval_jaxpr/dot_general | solution.py:24
  29.8 6.1 %fusion.31 = f32[2048,256]{0,1:T(8,128)} fusion(s32[2048]{0:T(1024)S(1)} %bitcast.55, bf16[4,2048,256]{2,1,0:T(8,128)(2,1)} %get-tuple-element.130, s32[]{:T(128)} %get-tuple-element.120), kind=kOutput, calls=%fused_computation.5.clone.1 | convolution fusion | flops 2151677952 | bytes 3154432 | tf_op jit(solution)/shard_map/while/body/eval_jaxpr/dot_general | solution.py:24
  35.9 5.8 %maximum_add_fusion.2 = f32[2048,512]{0,1:T(8,128)} fusion(f32[2048,256]{0,1:T(8,128)S(1)} %fusion.30, f32[2048,256]{0,1:T(8,128)} %fusion.31, f32[2048,512]{0,1:T(8,128)} %get-tuple-element.121, pred[]{:T(512)S(6)} %compare.5), kind=kLoop, calls=%fused_computation.9.clone.1 | loop fusion | flops 3145728 | bytes 12582913 | tf_op jit(solution)/shard_map/while/body/eval_jaxpr/add | solution.py:28
  41.6 0.8 constant_dynamic-slice_fusion.3
  42.5 4.8 %fusion.30 = f32[2048,256]{0,1:T(8,128)S(1)} fusion(s32[2048]{0:T(1024)S(1)} %bitcast.56, bf16[4,2048,256]{2,1,0:T(8,128)(2,1)} %get-tuple-element.130, s32[]{:T(128)} %get-tuple-element.120), kind=kOutput, calls=%fused_computation.6.clone.1 | convolution fusion | flops 2151677952 | bytes 3154432 | tf_op jit(solution)/shard_map/while/body/eval_jaxpr/dot_general | solution.py:24
  47.2 6.1 %fusion.31 = f32[2048,256]{0,1:T(8,128)} fusion(s32[2048]{0:T(1024)S(1)} %bitcast.55, bf16[4,2048,256]{2,1,0:T(8,128)(2,1)} %get-tuple-element.130, s32[]{:T(128)} %get-tuple-element.120), kind=kOutput, calls=%fused_computation.5.clone.1 | convolution fusion | flops 2151677952 | bytes 3154432 | tf_op jit(solution)/shard_map/while/body/eval_jaxpr/dot_general | solution.py:24
  53.3 5.8 %maximum_add_fusion.2 = f32[2048,512]{0,1:T(8,128)} fusion(f32[2048,256]{0,1:T(8,128)S(1)} %fusion.30, f32[2048,256]{0,1:T(8,128)} %fusion.31, f32[2048,512]{0,1:T(8,128)} %get-tuple-element.121, pred[]{:T(512)S(6)} %compare.5), kind=kLoop, calls=%fused_computation.9.clone.1 | loop fusion | flops 3145728 | bytes 12582913 | tf_op jit(solution)/shard_map/while/body/eval_jaxpr/add | solution.py:28
  59.1 0.8 constant_dynamic-slice_fusion.3
  59.9 4.8 %fusion.30 = f32[2048,256]{0,1:T(8,128)S(1)} fusion(s32[2048]{0:T(1024)S(1)} %bitcast.56, bf16[4,2048,256]{2,1,0:T(8,128)(2,1)} %get-tuple-element.130, s32[]{:T(128)} %get-tuple-element.120), kind=kOutput, calls=%fused_computation.6.clone.1 | convolution fusion | flops 2151677952 | bytes 3154432 | tf_op jit(solution)/shard_map/while/body/eval_jaxpr/dot_general | solution.py:24
  64.7 6.1 %fusion.31 = f32[2048,256]{0,1:T(8,128)} fusion(s32[2048]{0:T(1024)S(1)} %bitcast.55, bf16[4,2048,256]{2,1,0:T(8,128)(2,1)} %get-tuple-element.130, s32[]{:T(128)} %get-tuple-element.120), kind=kOutput, calls=%fused_computation.5.clone.1 | convolution fusion | flops 2151677952 | bytes 3154432 | tf_op jit(solution)/shard_map/while/body/eval_jaxpr/dot_general | solution.py:24
  70.8 5.8 %maximum_add_fusion.2 = f32[2048,512]{0,1:T(8,128)} fusion(f32[2048,256]{0,1:T(8,128)S(1)} %fusion.30, f32[2048,256]{0,1:T(8,128)} %fusion.31, f32[2048,512]{0,1:T(8,128)} %get-tuple-element.121, pred[]{:T(512)S(6)} %compare.5), kind=kLoop, calls=%fused_computation.9.clone.1 | loop fusion | flops 3145728 | bytes 12582913 | tf_op jit(solution)/shard_map/while/body/eval_jaxpr/add | solution.py:28
  76.6 5.3 %copy.13 = f32[2048,512]{1,0:T(8,128)} copy(f32[2048,512]{0,1:T(8,128)} %get-tuple-element.32) | data formatting | bytes 8388608 | tf_op jit(solution)/shard_map/while | solution.py:31
  81.9 5.0 %copy.14 = f32[8,16,16,512]{3,2,1,0:T(8,128)} copy(f32[8,16,16,512]{3,2,0,1:T(8,128)} %bitcast.52) | data formatting | bytes 8388608 | tf_op jit(solution)/shard_map/transpose | solution.py:65
  86.9 0.0 all-to-all-done
  86.9 10.8 %all-to-all-start.1 = ((f32[128,16,512]{2,1,0:T(8,128)}), f32[128,16,512]{2,1,0:T(8,128)}, u32[]{:S(2)}, u32[]{:S(2)}) async-start(f32[128,16,512]{2,1,0:T(8,128)} %bitcast.51), calls=%async_computation.1 | async-start | bytes 8388608 | tf_op jit(solution)/shard_map/all_to_all | solution.py:66
  97.7 0.1 all_to_all.16
  97.8 0.0 copy-start
  97.8 51.1 %all-to-all-done.1 = f32[128,16,512]{2,1,0:T(8,128)} async-done(((f32[128,16,512]{2,1,0:T(8,128)}), f32[128,16,512]{2,1,0:T(8,128)}, u32[]{:S(2)}, u32[]{:S(2)}) %all-to-all-start.1) | async-done | bytes 4194336 | tf_op jit(solution)/shard_map/all_to_all | solution.py:66
  148.8 2.6 %bitcast_reduce_fusion = f32[8,16,512]{2,1,0:T(8,128)S(1)} fusion(f32[128,16,512]{2,1,0:T(8,128)} %all-to-all-done.1), kind=kLoop, calls=%fused_computation.18 | loop fusion | flops 983040 | bytes 4456448 | tf_op jit(solution)/shard_map/reduce_sum | solution.py:67
  151.5 1.5 scatter_custom_fusion
  153.0 0.2 multiply_reduce_fusion.1
  153.2 1.5 scatter_custom_fusion.1
  154.8 0.2 multiply_reduce_fusion
  155.0 0.0 copy-done
  155.0 1.9 %fusion.13 = (f32[1,1024,256]{2,1,0:T(8,128)S(1)}, f32[1,1024,256]{2,1,0:T(8,128)S(1)}) fusion(f32[1024,256]{1,0:T(8,128)S(1)} %scatter_custom_fusion, f32[2,1024,256]{2,1,0:T(8,128)} %param.10, f32[1024]{0:T(1024)S(1)} %get-tuple-element.83, f32[1024]{0:T(1024)S(1)} %get-tuple-element.82, f32[1024,256]{1,0:T(8,128)S(1)} %scatter_custom_fusion.1), kind=kLoop, calls=%fused_computation.23 | loop fusion | flops 1572864 | bytes 6299648 | tf_op jit(solution)/shard_map/stack | solution.py:53
  156.9 1.5 pad_maximum_fusion
  158.4 0.6 pad_maximum_fusion.1
  (7 shorter events, 0.1 us)
Async XLA Ops:
  2.0 84.9 %all-to-all-start = ((s32[8,16,2]{1,2,0:T(2,128)}), s32[8,16,2]{1,2,0:T(2,128)S(1)}, u32[]{:S(2)}, u32[]{:S(2)}) async-start(s32[8,16,2]{1,2,0:T(2,128)} %copy.11), calls=%async_computation | async-start | bytes 16384 | tf_op jit(solution)/shard_map/all_to_all | solution.py:70
  86.9 62.0 %all-to-all-start.1 = ((f32[128,16,512]{2,1,0:T(8,128)}), f32[128,16,512]{2,1,0:T(8,128)}, u32[]{:S(2)}, u32[]{:S(2)}) async-start(f32[128,16,512]{2,1,0:T(8,128)} %bitcast.51), calls=%async_computation.1 | async-start | bytes 8388608 | tf_op jit(solution)/shard_map/all_to_all | solution.py:66
  97.8 57.2 %copy-start = (f32[2,1024]{1,0:T(2,128)S(1)}, f32[2,1024]{1,0:T(2,128)}, u32[]{:S(2)}) copy-start(f32[2,1024]{1,0:T(2,128)} %param.11) | copy-start | bytes 24580
where the time goes:
time: 160 us; the launch traced here: 159 us
  waiting for transfers between devices  51.1 us (32%)
  matrix products  43.5 us (27%)
  other arithmetic  31.9 us (20%)
  starting transfers between devices  16.8 us (10%)
  local copies, waits for them, and re-layouts  15 us (9%)
    all_to_all x1, waiting for transfers between devices, local(): lax.all_to_all(ordered, ('group', 'local'), split_axis=0, concat_axis=0,...  51.1 us
    dot_general x8, matrix products, accumulate(): lax.dot_general(onehot, gradients, (((0,), (0,)), ((), ())), preferred_el...  43.5 us
    add x4, other arithmetic, accumulate(): return (running + jnp.concatenate(pieces, axis=1), None)  21.8 us
    all_to_all x1, starting transfers between devices, local(): lax.all_to_all(ordered, ('group', 'local'), split_axis=0, concat_axis=0,...  10.8 us
    all_to_all x1, starting transfers between devices, local(): lax.all_to_all(row_pairs, 'group', split_axis=0, concat_axis=0, tiled=True)  5.97 us
    while x1, local copies, waits for them, and re-layouts, slot_sums(): summed, _ = lax.scan(accumulate, start_sums, (grad_blocks, index_blocks))  5.34 us
    transpose x1, local copies, waits for them, and re-layouts, local(): jnp.transpose(ordered, (1, 0, 2, 3)).reshape(n_local * slots, 2 * width)  4.95 us
    another operation x3, other arithmetic, apply_update(): return (jnp.stack(new_tables), jnp.stack(new_accums))  3.95 us
  transfers between devices with their start and end apart: 2, of which 1 were waited for; matrix products, arithmetic and copies ran while one was open for 50% of the time, Pallas kernels for 0%

commit v1 on v0

--- a/solution.py
+++ b/solution.py
@@ -5,6 +5,18 @@
 
 learning_rate = 0.1
 epsilon = 1e-08
+
+
+def in_blocks(array, dim, count):
+    shape = array.shape
+    parts = array.reshape(*shape[:dim], count, shape[dim] // count, *shape[dim + 1 :])
+    return jnp.moveaxis(parts, dim, 0)
+
+
+def laid_out(blocks, dim):
+    blocks = jnp.moveaxis(blocks, 0, dim)
+    shape = blocks.shape
+    return blocks.reshape(*shape[:dim], shape[dim] * shape[dim + 1], *shape[dim + 2 :])
 
 
 def slot_sums(lookup_grads, slot_index, row_count):
@@ -67,7 +79,15 @@
     arrived = jnp.sum(received.reshape(n_group, n_local, capacity, 2 * width), axis=1).reshape(
         slots, 2 * width
     )
-    arrived_rows = lax.all_to_all(row_pairs, "group", split_axis=0, concat_axis=0, tiled=True)
+    size, index = (lax.axis_size("group"), lax.axis_index("group"))
+    blocks = in_blocks(row_pairs, 0, size)
+    whole = blocks
+    for step in range(1, size):
+        target, source = ((index + step) % size, (index - step) % size)
+        sent = lax.dynamic_index_in_dim(blocks, target, 0)
+        other = lax.ppermute(sent, "group", [(i, (i + step) % size) for i in range(size)])
+        whole = lax.dynamic_update_slice_in_dim(whole, other, source, axis=0)
+    arrived_rows = laid_out(whole, 0)
     return apply_update(arrived, arrived_rows, tables, accums)
 
 

time: 160 us -> 142 us (0.89)
  other arithmetic: 31.9 us -> 16.1 us
  waiting for transfers between devices: 51.1 us -> 36.3 us
  starting transfers between devices: 16.8 us -> 26.3 us
  local copies, waits for them, and re-layouts: 15 us -> 21.8 us
  matrix products: 43.5 us -> 38.8 us
    all_to_all x1, waiting for transfers between devices: 51.1 us -> 3.97 us  [local(): lax.all_to_all(ordered, ('group', 'local'), split_axis=0, concat_axis=0,...]
    ppermute x0 -> x7, waiting for transfers between devices: none -> 32.4 us  [local(): lax.ppermute(sent, 'group', [(i, (i + step) % size) for i in range(size)])]
    add x4, other arithmetic: 21.8 us -> 5.96 us  [accumulate(): return (running + jnp.concatenate(pieces, axis=1), None)]
    ppermute x0 -> x7, starting transfers between devices: none -> 14.3 us  [local(): lax.ppermute(sent, 'group', [(i, (i + step) % size) for i in range(size)])]
    while x0 -> x16, local copies, waits for them, and re-layouts: none -> 7.9 us
    all_to_all x1 -> x0, starting transfers between devices: 5.97 us -> none  [local(): lax.all_to_all(row_pairs, 'group', split_axis=0, concat_axis=0, tiled=True)]
    dot_general x8, matrix products: 43.5 us -> 38.8 us  [accumulate(): lax.dot_general(onehot, gradients, (((0,), (0,)), ((), ())), preferred_el...]
  transfers between devices with their start and end apart: 2 -> 8, of which waited for: 1 -> 5; matrix products, arithmetic and copies ran while one was open for 50% -> 0% of each run, Pallas kernels for 0% -> 0%
where the time goes in v1:
time: 142 us; the launch traced here: 140 us
  matrix products  38.8 us (27%)
  waiting for transfers between devices  36.3 us (26%)
  starting transfers between devices  26.3 us (19%)
  local copies, waits for them, and re-layouts  21.8 us (15%)
  other arithmetic  16.1 us (11%)
    dot_general x8, matrix products, accumulate(): lax.dot_general(onehot, gradients, (((0,), (0,)), ((), ())), preferred_el...  38.8 us
    ppermute x7, waiting for transfers between devices, local(): lax.ppermute(sent, 'group', [(i, (i + step) % size) for i in range(size)])  32.4 us
    ppermute x7, starting transfers between devices, local(): lax.ppermute(sent, 'group', [(i, (i + step) % size) for i in range(size)])  14.3 us
    all_to_all x1, starting transfers between devices, local(): lax.all_to_all(ordered, ('group', 'local'), split_axis=0, concat_axis=0,...  12 us
    while x16, local copies, waits for them, and re-layouts  7.9 us
    add x4, other arithmetic, accumulate(): return (running + jnp.concatenate(pieces, axis=1), None)  5.96 us
    while x1, local copies, waits for them, and re-layouts, slot_sums(): summed, _ = lax.scan(accumulate, start_sums, (grad_blocks, index_blocks))  5.35 us
    transpose x1, local copies, waits for them, and re-layouts, local(): jnp.transpose(ordered, (1, 0, 2, 3)).reshape(n_local * slots, 2 * width)  5 us
  transfers between devices with their start and end apart: 8, of which 5 were waited for; matrix products, arithmetic and copies ran while one was open for 0% of the time, Pallas kernels for 0%

profile of v1, /device:TPU:1, one launch (start us, length us, event | category | flops | bytes accessed | tf_op | source)
XLA Modules:
  0.0 140.4 jit_solution(5652026241309643232)
XLA Ops:
  0.6 56.1 %while.12 = (s32[]{:T(128)}, f32[2048,512]{0,1:T(8,128)}, s32[4,2,2048]{2,1,0:T(2,128)}, bf16[4,2048,256]{2,1,0:T(8,128)(2,1)}, s32[]{:T(128)}, /*index=5*/s32[]{:T(128)}, s32[]{}) while((s32[]{:T(128)}, f32[2048,512]{0,1:T(8,128)}, s32[4,2,2048]{2,1,0:T(2,128)}, bf16[4,2048,256]{2,1,0:T(8,128)(2,1)}, s32[]{:T(128)}, ...), condition=%wide.region_1.2_spmd.clone.clone, body=%wide.region_0.1_spmd.clone.clone.sunk | while | flops 4306501632 | bytes 52478128 | solution.py:43
  0.7 0.8 constant_dynamic-slice_fusion.10
  1.5 4.8 %fusion.31 = f32[2048,256]{0,1:T(8,128)S(1)} fusion(s32[2048]{0:T(1024)S(1)} %bitcast.56, bf16[4,2048,256]{2,1,0:T(8,128)(2,1)} %get-tuple-element.137, s32[]{:T(128)S(6)} %copy.18), kind=kOutput, calls=%fused_computation.5.clone.1 | convolution fusion | flops 2151677952 | bytes 3153924 | tf_op jit(solution)/shard_map/while/body/eval_jaxpr/dot_general | solution.py:36
  6.3 0.0 copy-start
  6.3 4.9 %fusion.30 = f32[2048,256]{0,1:T(8,128)S(1)} fusion(s32[2048]{0:T(1024)S(1)} %bitcast.55, bf16[4,2048,256]{2,1,0:T(8,128)(2,1)} %get-tuple-element.137, s32[]{:T(128)S(6)} %copy.18), kind=kOutput, calls=%fused_computation.6.clone.1 | convolution fusion | flops 2151677952 | bytes 3153924 | tf_op jit(solution)/shard_map/while/body/eval_jaxpr/dot_general | solution.py:36
  11.2 0.0 copy-done
  11.2 1.5 %maximum_add_fusion.2 = f32[2048,512]{0,1:T(8,128)S(1)} fusion(f32[2048,256]{0,1:T(8,128)S(1)} %fusion.30, f32[2048,256]{0,1:T(8,128)S(1)} %fusion.31, f32[2048,512]{0,1:T(8,128)S(1)} %copy-done, pred[]{:T(512)S(6)} %compare.19), kind=kLoop, calls=%fused_computation.9.clone.1 | loop fusion | flops 3145728 | bytes 12582913 | tf_op jit(solution)/shard_map/while/body/eval_jaxpr/add | solution.py:40
  12.7 0.0 copy-start.1
  12.7 2.0 %copy-done.1 = f32[2048,512]{0,1:T(8,128)} copy-done((f32[2048,512]{0,1:T(8,128)}, f32[2048,512]{0,1:T(8,128)S(1)}, u32[]{:S(2)}) %copy-start.1) | copy-done | bytes 4194328 | tf_op jit(solution)/shard_map/while
  14.7 0.8 constant_dynamic-slice_fusion.10
  15.5 4.8 %fusion.31 = f32[2048,256]{0,1:T(8,128)S(1)} fusion(s32[2048]{0:T(1024)S(1)} %bitcast.56, bf16[4,2048,256]{2,1,0:T(8,128)(2,1)} %get-tuple-element.137, s32[]{:T(128)S(6)} %copy.18), kind=kOutput, calls=%fused_computation.5.clone.1 | convolution fusion | flops 2151677952 | bytes 3153924 | tf_op jit(solution)/shard_map/while/body/eval_jaxpr/dot_general | solution.py:36
  20.3 0.0 copy-start
  20.3 4.9 %fusion.30 = f32[2048,256]{0,1:T(8,128)S(1)} fusion(s32[2048]{0:T(1024)S(1)} %bitcast.55, bf16[4,2048,256]{2,1,0:T(8,128)(2,1)} %get-tuple-element.137, s32[]{:T(128)S(6)} %copy.18), kind=kOutput, calls=%fused_computation.6.clone.1 | convolution fusion | flops 2151677952 | bytes 3153924 | tf_op jit(solution)/shard_map/while/body/eval_jaxpr/dot_general | solution.py:36
  25.2 0.0 copy-done
  25.2 1.5 %maximum_add_fusion.2 = f32[2048,512]{0,1:T(8,128)S(1)} fusion(f32[2048,256]{0,1:T(8,128)S(1)} %fusion.30, f32[2048,256]{0,1:T(8,128)S(1)} %fusion.31, f32[2048,512]{0,1:T(8,128)S(1)} %copy-done, pred[]{:T(512)S(6)} %compare.19), kind=kLoop, calls=%fused_computation.9.clone.1 | loop fusion | flops 3145728 | bytes 12582913 | tf_op jit(solution)/shard_map/while/body/eval_jaxpr/add | solution.py:40
  26.7 0.0 copy-start.1
  26.7 2.0 %copy-done.1 = f32[2048,512]{0,1:T(8,128)} copy-done((f32[2048,512]{0,1:T(8,128)}, f32[2048,512]{0,1:T(8,128)S(1)}, u32[]{:S(2)}) %copy-start.1) | copy-done | bytes 4194328 | tf_op jit(solution)/shard_map/while
  28.7 0.8 constant_dynamic-slice_fusion.10
  29.5 4.8 %fusion.31 = f32[2048,256]{0,1:T(8,128)S(1)} fusion(s32[2048]{0:T(1024)S(1)} %bitcast.56, bf16[4,2048,256]{2,1,0:T(8,128)(2,1)} %get-tuple-element.137, s32[]{:T(128)S(6)} %copy.18), kind=kOutput, calls=%fused_computation.5.clone.1 | convolution fusion | flops 2151677952 | bytes 3153924 | tf_op jit(solution)/shard_map/while/body/eval_jaxpr/dot_general | solution.py:36
  34.3 0.0 copy-start
  34.3 4.9 %fusion.30 = f32[2048,256]{0,1:T(8,128)S(1)} fusion(s32[2048]{0:T(1024)S(1)} %bitcast.55, bf16[4,2048,256]{2,1,0:T(8,128)(2,1)} %get-tuple-element.137, s32[]{:T(128)S(6)} %copy.18), kind=kOutput, calls=%fused_computation.6.clone.1 | convolution fusion | flops 2151677952 | bytes 3153924 | tf_op jit(solution)/shard_map/while/body/eval_jaxpr/dot_general | solution.py:36
  39.2 0.0 copy-done
  39.2 1.5 %maximum_add_fusion.2 = f32[2048,512]{0,1:T(8,128)S(1)} fusion(f32[2048,256]{0,1:T(8,128)S(1)} %fusion.30, f32[2048,256]{0,1:T(8,128)S(1)} %fusion.31, f32[2048,512]{0,1:T(8,128)S(1)} %copy-done, pred[]{:T(512)S(6)} %compare.19), kind=kLoop, calls=%fused_computation.9.clone.1 | loop fusion | flops 3145728 | bytes 12582913 | tf_op jit(solution)/shard_map/while/body/eval_jaxpr/add | solution.py:40
  40.7 0.0 copy-start.1
  40.8 2.0 %copy-done.1 = f32[2048,512]{0,1:T(8,128)} copy-done((f32[2048,512]{0,1:T(8,128)}, f32[2048,512]{0,1:T(8,128)S(1)}, u32[]{:S(2)}) %copy-start.1) | copy-done | bytes 4194328 | tf_op jit(solution)/shard_map/while
  42.7 0.8 constant_dynamic-slice_fusion.10
  43.5 4.8 %fusion.31 = f32[2048,256]{0,1:T(8,128)S(1)} fusion(s32[2048]{0:T(1024)S(1)} %bitcast.56, bf16[4,2048,256]{2,1,0:T(8,128)(2,1)} %get-tuple-element.137, s32[]{:T(128)S(6)} %copy.18), kind=kOutput, calls=%fused_computation.5.clone.1 | convolution fusion | flops 2151677952 | bytes 3153924 | tf_op jit(solution)/shard_map/while/body/eval_jaxpr/dot_general | solution.py:36
  48.3 0.0 copy-start
  48.3 4.9 %fusion.30 = f32[2048,256]{0,1:T(8,128)S(1)} fusion(s32[2048]{0:T(1024)S(1)} %bitcast.55, bf16[4,2048,256]{2,1,0:T(8,128)(2,1)} %get-tuple-element.137, s32[]{:T(128)S(6)} %copy.18), kind=kOutput, calls=%fused_computation.6.clone.1 | convolution fusion | flops 2151677952 | bytes 3153924 | tf_op jit(solution)/shard_map/while/body/eval_jaxpr/dot_general | solution.py:36
  53.3 0.0 copy-done
  53.3 1.5 %maximum_add_fusion.2 = f32[2048,512]{0,1:T(8,128)S(1)} fusion(f32[2048,256]{0,1:T(8,128)S(1)} %fusion.30, f32[2048,256]{0,1:T(8,128)S(1)} %fusion.31, f32[2048,512]{0,1:T(8,128)S(1)} %copy-done, pred[]{:T(512)S(6)} %compare.19), kind=kLoop, calls=%fused_computation.9.clone.1 | loop fusion | flops 3145728 | bytes 12582913 | tf_op jit(solution)/shard_map/while/body/eval_jaxpr/add | solution.py:40
  54.8 0.0 copy-start.1
  54.8 2.0 %copy-done.1 = f32[2048,512]{0,1:T(8,128)} copy-done((f32[2048,512]{0,1:T(8,128)}, f32[2048,512]{0,1:T(8,128)S(1)}, u32[]{:S(2)}) %copy-start.1) | copy-done | bytes 4194328 | tf_op jit(solution)/shard_map/while
  56.7 5.3 %copy.7 = f32[2048,512]{1,0:T(8,128)} copy(f32[2048,512]{0,1:T(8,128)} %get-tuple-element.32) | data formatting | bytes 8388608 | tf_op jit(solution)/shard_map/while | solution.py:43
  62.1 5.0 %copy.8 = f32[8,16,16,512]{3,2,1,0:T(8,128)} copy(f32[8,16,16,512]{3,2,0,1:T(8,128)} %bitcast.52) | data formatting | bytes 8388608 | tf_op jit(solution)/shard_map/transpose | solution.py:77
  67.1 12.0 %all-to-all-start = ((f32[128,16,512]{2,1,0:T(8,128)}), f32[128,16,512]{2,1,0:T(8,128)}, u32[]{:S(2)}, u32[]{:S(2)}) async-start(f32[128,16,512]{2,1,0:T(8,128)} %bitcast.51), calls=%async_computation | async-start | bytes 8388608 | tf_op jit(solution)/shard_map/all_to_all | solution.py:78
  79.2 0.0 copy-done.3
  79.2 0.1 reshape.77
  79.3 1.2 collective-permute-start.6
  80.4 1.9 %collective-permute-start.5 = (s32[1,16,2]{1,0,2:T(1,128)S(1)}, s32[1,16,2]{1,0,2:T(1,128)S(1)}, u32[]{:S(2)}, u32[]{:S(2)}) collective-permute-start(s32[1,16,2]{1,0,2:T(1,128)S(1)} %get-tuple-element.81), channel_id=1, source_target_pairs={{0,96},{16,112},{32,0},{48,16},{64,32},{80,48},{96,64},{112,80},{1... | collective-permute-start | bytes 392 | tf_op jit(solution)/shard_map/ppermute | solution.py:88
  82.3 1.0 collective-permute-start.4
  83.3 1.2 collective-permute-start.1
  84.5 1.0 collective-permute-start
  85.5 26.4 %collective-permute-done = s32[1,16,2]{1,0,2:T(1,128)S(1)} collective-permute-done((s32[1,16,2]{1,0,2:T(1,128)S(1)}, s32[1,16,2]{1,0,2:T(1,128)S(1)}, u32[]{:S(2)}, u32[]{:S(2)}) %collective-permute-start) | collective-permute-done | bytes 160 | tf_op jit(solution)/shard_map/ppermute | solution.py:88
  111.9 5.7 %collective-permute-start.2 = (s32[1,16,2]{1,0,2:T(1,128)S(1)}, s32[1,16,2]{1,0,2:T(1,128)S(1)}, u32[]{:S(2)}, u32[]{:S(2)}) collective-permute-start(s32[1,16,2]{1,0,2:T(1,128)S(1)} %get-tuple-element.84), channel_id=1, source_target_pairs={{0,48},{16,64},{32,80},{48,96},{64,112},{80,0},{96,16},{112,32},{1... | collective-permute-start | bytes 392 | tf_op jit(solution)/shard_map/ppermute | solution.py:88
  117.6 0.0 collective-permute-done.1
  117.6 2.4 %collective-permute-start.3 = (s32[1,16,2]{1,0,2:T(1,128)S(1)}, s32[1,16,2]{1,0,2:T(1,128)S(1)}, u32[]{:S(2)}, u32[]{:S(2)}) collective-permute-start(s32[1,16,2]{1,0,2:T(1,128)S(1)} %get-tuple-element.83), channel_id=1, source_target_pairs={{0,64},{16,80},{32,96},{48,112},{64,0},{80,16},{96,32},{112,48},{1... | collective-permute-start | bytes 392 | tf_op jit(solution)/shard_map/ppermute | solution.py:88
  120.1 0.5 collective-permute-done.2
  120.6 2.6 %collective-permute-done.3 = s32[1,16,2]{1,0,2:T(1,128)S(1)} collective-permute-done((s32[1,16,2]{1,0,2:T(1,128)S(1)}, s32[1,16,2]{1,0,2:T(1,128)S(1)}, u32[]{:S(2)}, u32[]{:S(2)}) %collective-permute-start.3) | collective-permute-done | bytes 160 | tf_op jit(solution)/shard_map/ppermute | solution.py:88
  123.2 0.0 collective-permute-done.4
  123.2 0.0 collective-permute-done.5
  123.3 2.8 %collective-permute-done.6 = s32[1,16,2]{1,0,2:T(1,128)S(1)} collective-permute-done((s32[1,16,2]{1,0,2:T(1,128)S(1)}, s32[1,16,2]{1,0,2:T(1,128)S(1)}, u32[]{:S(2)}, u32[]{:S(2)}) %collective-permute-start.6) | collective-permute-done | bytes 160 | tf_op jit(solution)/shard_map/ppermute | solution.py:88
  126.2 0.1 reshape.78
  126.3 0.0 copy-start.2
  126.3 4.0 %all-to-all-done = f32[128,16,512]{2,1,0:T(8,128)} async-done(((f32[128,16,512]{2,1,0:T(8,128)}), f32[128,16,512]{2,1,0:T(8,128)}, u32[]{:S(2)}, u32[]{:S(2)}) %all-to-all-start) | async-done | bytes 4194336 | tf_op jit(solution)/shard_map/all_to_all | solution.py:78
  130.2 2.6 %bitcast_reduce_fusion = f32[8,16,512]{2,1,0:T(8,128)S(1)} fusion(f32[128,16,512]{2,1,0:T(8,128)} %all-to-all-done), kind=kLoop, calls=%fused_computation.18 | loop fusion | flops 983040 | bytes 4456448 | tf_op jit(solution)/shard_map/reduce_sum | solution.py:79
  132.9 1.5 %scatter_custom_fusion.1 = f32[1024,256]{1,0:T(8,128)S(1)} fusion(s32[128]{0:T(128)S(1)} %get-tuple-element.88, f32[]{:T(128)} %constant.133.clone.1, f32[128,512]{1,0:T(8,128)S(1)} %bitcast.53), kind=kCustom, calls=%fused_computation.26 | custom fusion | flops 32768 | bytes 1179652 | tf_op jit(solution)/shard_map/scatter-add | solution.py:57
  134.4 0.2 multiply_reduce_fusion
  134.6 1.5 %scatter_custom_fusion = f32[1024,256]{1,0:T(8,128)S(1)} fusion(s32[128]{0:T(128)S(1)} %get-tuple-element.87, f32[]{:T(128)} %constant.133.clone.1, f32[128,512]{1,0:T(8,128)S(1)} %bitcast.54), kind=kCustom, calls=%fused_computation.28 | custom fusion | flops 32768 | bytes 1179652 | tf_op jit(solution)/shard_map/scatter-add | solution.py:57
  136.2 0.2 multiply_reduce_fusion.1
  136.4 0.0 copy-done.2
  136.4 0.6 pad_maximum_fusion.1
  137.0 1.9 %fusion.13 = (f32[1,1024,256]{2,1,0:T(8,128)S(1)}, f32[1,1024,256]{2,1,0:T(8,128)S(1)}) fusion(f32[1024,256]{1,0:T(8,128)S(1)} %scatter_custom_fusion, f32[2,1024,256]{2,1,0:T(8,128)} %param.10, f32[1024]{0:T(1024)S(1)} %get-tuple-element.90, f32[1024]{0:T(1024)S(1)} %get-tuple-element.89, f32[1024,256]{1,0:T(8,128)S(1)} %scatter_custom_fusion.1), kind=kLoop, calls=%fused_computation.23 | loop fusion | flops 1572864 | bytes 6299648 | tf_op jit(solution)/shard_map/stack | solution.py:65
  138.9 1.5 %pad_maximum_fusion = f32[2,1024,256]{2,1,0:T(8,128)} fusion(f32[1,1024,256]{2,1,0:T(8,128)S(1)} %get-tuple-element.75, f32[1,1024,256]{2,1,0:T(8,128)S(1)} %get-tuple-element.74), kind=kLoop, calls=%fused_computation.19 | loop fusion | flops 524288 | bytes 4194304 | tf_op jit(solution)/shard_map/stack | solution.py:65
  (15 shorter events, 0.2 us)
Async XLA Ops:
  6.3 4.9 %copy-start = (f32[2048,512]{0,1:T(8,128)S(1)}, f32[2048,512]{0,1:T(8,128)}, u32[]{:S(2)}) copy-start(f32[2048,512]{0,1:T(8,128)} %get-tuple-element.128) | copy-start | bytes 12582916 | tf_op jit(solution)/shard_map/while
  12.7 2.0 %copy-start.1 = (f32[2048,512]{0,1:T(8,128)}, f32[2048,512]{0,1:T(8,128)S(1)}, u32[]{:S(2)}) copy-start(f32[2048,512]{0,1:T(8,128)S(1)} %maximum_add_fusion.2) | copy-start | bytes 12582916 | tf_op jit(solution)/shard_map/while
  20.3 4.9 %copy-start = (f32[2048,512]{0,1:T(8,128)S(1)}, f32[2048,512]{0,1:T(8,128)}, u32[]{:S(2)}) copy-start(f32[2048,512]{0,1:T(8,128)} %get-tuple-element.128) | copy-start | bytes 12582916 | tf_op jit(solution)/shard_map/while
  26.7 2.0 %copy-start.1 = (f32[2048,512]{0,1:T(8,128)}, f32[2048,512]{0,1:T(8,128)S(1)}, u32[]{:S(2)}) copy-start(f32[2048,512]{0,1:T(8,128)S(1)} %maximum_add_fusion.2) | copy-start | bytes 12582916 | tf_op jit(solution)/shard_map/while
  34.3 4.9 %copy-start = (f32[2048,512]{0,1:T(8,128)S(1)}, f32[2048,512]{0,1:T(8,128)}, u32[]{:S(2)}) copy-start(f32[2048,512]{0,1:T(8,128)} %get-tuple-element.128) | copy-start | bytes 12582916 | tf_op jit(solution)/shard_map/while
  40.7 2.0 %copy-start.1 = (f32[2048,512]{0,1:T(8,128)}, f32[2048,512]{0,1:T(8,128)S(1)}, u32[]{:S(2)}) copy-start(f32[2048,512]{0,1:T(8,128)S(1)} %maximum_add_fusion.2) | copy-start | bytes 12582916 | tf_op jit(solution)/shard_map/while
  48.3 4.9 %copy-start = (f32[2048,512]{0,1:T(8,128)S(1)}, f32[2048,512]{0,1:T(8,128)}, u32[]{:S(2)}) copy-start(f32[2048,512]{0,1:T(8,128)} %get-tuple-element.128) | copy-start | bytes 12582916 | tf_op jit(solution)/shard_map/while
  54.8 2.0 %copy-start.1 = (f32[2048,512]{0,1:T(8,128)}, f32[2048,512]{0,1:T(8,128)S(1)}, u32[]{:S(2)}) copy-start(f32[2048,512]{0,1:T(8,128)S(1)} %maximum_add_fusion.2) | copy-start | bytes 12582916 | tf_op jit(solution)/shard_map/while
  67.1 12.1 %copy-start.3 = (s32[2,128]{1,0:T(2,128)S(1)}, s32[2,128]{1,0:T(2,128)}, u32[]{:S(2)}) copy-start(s32[2,128]{1,0:T(2,128)} %param.9) | copy-start | bytes 3076
  67.1 63.1 %all-to-all-start = ((f32[128,16,512]{2,1,0:T(8,128)}), f32[128,16,512]{2,1,0:T(8,128)}, u32[]{:S(2)}, u32[]{:S(2)}) async-start(f32[128,16,512]{2,1,0:T(8,128)} %bitcast.51), calls=%async_computation | async-start | bytes 8388608 | tf_op jit(solution)/shard_map/all_to_all | solution.py:78
  79.3 46.9 %collective-permute-start.6 = (s32[1,16,2]{1,0,2:T(1,128)S(1)}, s32[1,16,2]{1,0,2:T(1,128)S(1)}, u32[]{:S(2)}, u32[]{:S(2)}) collective-permute-start(s32[1,16,2]{1,0,2:T(1,128)S(1)} %get-tuple-element.80), channel_id=1, source_target_pairs={{0,112},{16,0},{32,16},{48,32},{64,48},{80,64},{96,80},{112,96},{1... | collective-permute-start | bytes 392 | tf_op jit(solution)/shard_map/ppermute | solution.py:88
  80.4 42.8 %collective-permute-start.5 = (s32[1,16,2]{1,0,2:T(1,128)S(1)}, s32[1,16,2]{1,0,2:T(1,128)S(1)}, u32[]{:S(2)}, u32[]{:S(2)}) collective-permute-start(s32[1,16,2]{1,0,2:T(1,128)S(1)} %get-tuple-element.81), channel_id=1, source_target_pairs={{0,96},{16,112},{32,0},{48,16},{64,32},{80,48},{96,64},{112,80},{1... | collective-permute-start | bytes 392 | tf_op jit(solution)/shard_map/ppermute | solution.py:88
  82.3 40.9 %collective-permute-start.4 = (s32[1,16,2]{1,0,2:T(1,128)S(1)}, s32[1,16,2]{1,0,2:T(1,128)S(1)}, u32[]{:S(2)}, u32[]{:S(2)}) collective-permute-start(s32[1,16,2]{1,0,2:T(1,128)S(1)} %get-tuple-element.82), channel_id=1, source_target_pairs={{0,80},{16,96},{32,112},{48,0},{64,16},{80,32},{96,48},{112,64},{1... | collective-permute-start | bytes 392 | tf_op jit(solution)/shard_map/ppermute | solution.py:88
  83.3 34.3 %collective-permute-start.1 = (s32[1,16,2]{1,0,2:T(1,128)S(1)}, s32[1,16,2]{1,0,2:T(1,128)S(1)}, u32[]{:S(2)}, u32[]{:S(2)}) collective-permute-start(s32[1,16,2]{1,0,2:T(1,128)S(1)} %get-tuple-element.85), channel_id=1, source_target_pairs={{0,32},{16,48},{32,64},{48,80},{64,96},{80,112},{96,0},{112,16},{1... | collective-permute-start | bytes 392 | tf_op jit(solution)/shard_map/ppermute | solution.py:88
  84.5 27.4 %collective-permute-start = (s32[1,16,2]{1,0,2:T(1,128)S(1)}, s32[1,16,2]{1,0,2:T(1,128)S(1)}, u32[]{:S(2)}, u32[]{:S(2)}) collective-permute-start(s32[1,16,2]{1,0,2:T(1,128)S(1)} %get-tuple-element.86), channel_id=1, source_target_pairs={{0,16},{16,32},{32,48},{48,64},{64,80},{80,96},{96,112},{112,0},{1... | collective-permute-start | bytes 392 | tf_op jit(solution)/shard_map/ppermute | solution.py:88
  111.9 8.6 %collective-permute-start.2 = (s32[1,16,2]{1,0,2:T(1,128)S(1)}, s32[1,16,2]{1,0,2:T(1,128)S(1)}, u32[]{:S(2)}, u32[]{:S(2)}) collective-permute-start(s32[1,16,2]{1,0,2:T(1,128)S(1)} %get-tuple-element.84), channel_id=1, source_target_pairs={{0,48},{16,64},{32,80},{48,96},{64,112},{80,0},{96,16},{112,32},{1... | collective-permute-start | bytes 392 | tf_op jit(solution)/shard_map/ppermute | solution.py:88
  117.6 5.6 %collective-permute-start.3 = (s32[1,16,2]{1,0,2:T(1,128)S(1)}, s32[1,16,2]{1,0,2:T(1,128)S(1)}, u32[]{:S(2)}, u32[]{:S(2)}) collective-permute-start(s32[1,16,2]{1,0,2:T(1,128)S(1)} %get-tuple-element.83), channel_id=1, source_target_pairs={{0,64},{16,80},{32,96},{48,112},{64,0},{80,16},{96,32},{112,48},{1... | collective-permute-start | bytes 392 | tf_op jit(solution)/shard_map/ppermute | solution.py:88
  126.3 10.1 %copy-start.2 = (f32[2,1024]{1,0:T(2,128)S(1)}, f32[2,1024]{1,0:T(2,128)}, u32[]{:S(2)}) copy-start(f32[2,1024]{1,0:T(2,128)} %param.11) | copy-start | bytes 24580
